TPU v7x, 32 devices: a whole 2x2x4 slice. The times are simulated.
32 devices in a mesh: wide: 8 (over y, x, core), quad: 4 (over z).
Axes of the slice: x: 2, y: 2, z: 4, core: 2. Of those that a mesh axis runs over, the one named last changes fastest.
Arguments:
- basis: float32 [16, 2097152], P(None, ('wide', 'quad')), may hold values from -6 to 6
- target: float32 [2097152], P(('wide', 'quad')), may hold values from -6 to 6
- sign_bits: int32 [2097152], P(('wide', 'quad')), may hold values from 0 to 1
- samples: int32 [8192], replicated, may hold values from 0 to 2097151
- owners: int32 [8192], replicated, may hold values from 0 to 7
Outputs:
- sketch: float32 [8192, 17], P(('wide', 'quad'))
- gram: float32 [8, 16, 17], P('quad')
Inputs may be any that keep to these rules, and one draw needn't show every extreme that they name: `samples`: sampled scenarios may repeat.
All inputs are finite; a program needn't handle non-finite values.
Results may differ from a plain program's by a relative error of at most 0.0003.
Values sent between devices are 32-bit elements; how exact they have to be, the bound alone decides.
A program may use at most 128 MiB of HBM per device.

v0:
```python
import functools
import math

import jax
import jax.numpy as jnp
from jax import lax
from jax.experimental import pallas as pl
from jax.experimental.pallas import tpu as pltpu
from jax.sharding import PartitionSpec as P

GROUPS = 8
LANES = 128
LINE = 256
HIGH = 8
SLOT = 32
MESH = pl.DeviceIdType.MESH


def bits_of(n):
    return n.bit_length() - 1


def parity(x, nbits):
    shift = 1
    while shift < nbits:
        x = x ^ (x >> shift)
        shift *= 2
    return x & 1


def butterfly(parts):
    half = 1
    while half < len(parts):
        for at in range(0, len(parts), 2 * half):
            for i in range(at, at + half):
                parts[i], parts[i + half] = parts[i] + parts[i + half], parts[i] - parts[i + half]
        half *= 2
    return parts


def place_of(high):
    return ((high & 1) * (HIGH // 2) + (high >> 1)) * SLOT


def split(x):
    top = x.astype(jnp.bfloat16)
    return top, (x - top.astype(jnp.float32)).astype(jnp.bfloat16)


def contract_last(a, b, **kw):
    return lax.dot_general(a, b, (((1,), (1,)), ((), ())), preferred_element_type=jnp.float32, **kw)


def sketch_kernel(
    n_wide, n_quad, scale, samp, owners, bits_in, x_in, t_in, sketch, gram,
    bits_all, x_all, t_all, load_sems,
    field, table, walsh, unit, picks, picks_a, picks_b, rows_a, rows_b, sems,
    main, last, got_main, got_last, sum_main, sum_last, wide_main, wide_last,
    row_main, row_last, quad_main, quad_last, wide_gram, own_gram, quad_gram,
    mate_sends, mate_recvs, chip_sends, chip_recvs, sends, recvs
):
    chunk = x_all.shape[2]
    lines_in = chunk // LANES
    mids = chunk // LINE
    local_bits = bits_of(HIGH * chunk)
    devices, cols, per_dev = main.shape
    lines = per_dev // LANES
    wide = lax.axis_index("wide")
    quad = lax.axis_index("quad")
    me = wide * n_quad + quad
    core, chip, chips = wide % 2, wide // 2, n_wide // 2
    mate = (wide + 1 - 2 * core, quad)
    wide_peers = [((wide + k) % n_wide, quad) for k in range(1, n_wide)]
    quad_peers = [(wide, (quad + k) % n_quad) for k in range(1, n_quad)]
    barrier = pltpu.get_barrier_semaphore()

    def loads(h):
        at = pl.multiple_of(h * chunk, chunk)
        rows = pl.ds(pl.multiple_of(h * lines_in, lines_in), lines_in)
        return (
            pltpu.make_async_copy(bits_in.at[rows], bits_all.at[h], load_sems.at[0, h]),
            pltpu.make_async_copy(t_in.at[rows], t_all.at[h], load_sems.at[1, h]),
            pltpu.make_async_copy(x_in.at[:, pl.ds(at, chunk)], x_all.at[h], load_sems.at[2, h]),
        )

    for h in range(HIGH):
        for copy in loads(h):
            copy.start()
    for peer in wide_peers + quad_peers:
        pl.semaphore_signal(barrier, inc=1, device_id=peer, device_id_type=MESH)
    a = lax.broadcasted_iota(jnp.int32, (LINE, LINE), 0)
    b = lax.broadcasted_iota(jnp.int32, (LINE, LINE), 1)
    line = (1 - 2 * parity(a & b, bits_of(LINE))).astype(jnp.float32).astype(jnp.bfloat16)
    walsh[:, :LINE] = line
    walsh[:, LINE:] = line
    a = lax.broadcasted_iota(jnp.int32, (LANES, LANES), 0)
    b = lax.broadcasted_iota(jnp.int32, (LANES, LANES), 1)
    line = jnp.where(a == b, 1.0, 0.0).astype(jnp.bfloat16)
    unit[:, :LANES] = line
    unit[:, LANES:] = line
    picks[...] = samp[...] & (table.shape[0] - 1)

    row = lax.broadcasted_iota(jnp.int32, (8, LANES), 0)

    def first_pass(high, carry):
        for copy in loads(high):
            copy.wait()
        bits, t, x = bits_all.at[high], t_all.at[high], x_all.at[high]
        base = pl.multiple_of(place_of(high), SLOT)
        for part in range(LINE // LANES):
            for tile in range(cols // 8 + 1):
                values = []
                for mid in range(mids):
                    line = mid * (LINE // LANES) + part
                    flip = (1 - 2 * bits[line : line + 1, :]).astype(jnp.float32)
                    if tile < cols // 8:
                        value = x[tile * 8 : tile * 8 + 8, line * LANES : (line + 1) * LANES] * flip
                    else:
                        value = jnp.where(row == 0, t[line : line + 1, :] * flip, 0.0)
                    values.append(value)
                for mid, value in enumerate(butterfly(values)):
                    field[mid, pl.ds(base + tile * 8, 8), part * LANES : (part + 1) * LANES] = value
        return carry

    lax.fori_loop(0, HIGH, first_pass, 0)
    used = cols + 8

    def mix(mid, carry):
        halves = []
        for part in range(LINE // LANES):
            values = [
                field[mid, place_of(h) : place_of(h) + used, part * LANES : (part + 1) * LANES]
                for h in range(HIGH)
            ]
            values = butterfly(values)
            order = sorted(range(HIGH), key=place_of)
            blank = jnp.zeros((SLOT - used, LANES), jnp.float32)
            halves.append(jnp.concatenate([p for h in order for p in (values[h], blank)], axis=0))
        both = jnp.concatenate(split(jnp.concatenate(halves, axis=1)), axis=1)
        out = contract_last(walsh[...], both)
        at = pl.multiple_of(mid * LINE, LINE)
        table[pl.ds(at, LINE), :] = out[:, :LANES]
        table[pl.ds(at + mids * LINE, LINE), :] = out[:, LANES:]
        return carry

    lax.fori_loop(0, mids, mix, 0, unroll=8)
    table_rows = table.shape[0]
    half = devices // 2

    def chip_at(k):
        return (chip + 1 + k) % chips

    def device_at(slot):
        to_core = (core + 1 + slot // half) % 2
        to_wide = chip_at(slot // n_quad % chips) * 2 + to_core
        return to_wide * n_quad + slot % n_quad

    def fetch(slot, slots, sem):
        slot = jnp.minimum(slot, devices - 1)
        return pltpu.make_async_copy(picks.at[device_at(slot)], slots, sems.at[sem])

    def gather(slots, rows):
        for r in range(per_dev):
            rows[r : r + 1, :] = table[pl.ds(slots[r // LANES, r % LANES], 1), :]

    def finish(slot, rows):
        dev = device_at(slot)
        out = contract_last(unit[...], jnp.concatenate(split(rows[...]), axis=1))
        number = jnp.concatenate([samp[dev, i : i + 1] for i in range(lines)], axis=1)
        group = (number >> bits_of(table_rows)) & (LANES // SLOT - 1)
        sign = parity((number >> local_bits) & me, bits_of(devices))
        sign = (1 - 2 * sign).astype(jnp.float32) * scale
        total = jnp.zeros((used, per_dev), jnp.float32)
        for g in range(LANES // SLOT):
            total = jnp.where(group == g, out[g * SLOT : g * SLOT + used, :], total)
        total = total * sign
        main[slot] = total[:cols]
        for i in range(lines):
            last[pl.ds(slot * lines + i, 1), :] = total[cols : cols + 1, i * LANES : (i + 1) * LANES]

    def remote(src, dst, send_sem, recv_sem, peer):
        return pltpu.make_async_remote_copy(
            src_ref=src, dst_ref=dst, send_sem=send_sem, recv_sem=recv_sem,
            device_id=peer, device_id_type=MESH,
        )

    tall = n_quad * lines

    def group_of(k):
        return pl.ds(k * n_quad, n_quad), pl.ds(pl.multiple_of(k * tall, 8), tall)

    def mate_copies(k):
        at, at_last = group_of(k)
        return (
            remote(main.at[at], got_main.at[at], mate_sends.at[k], mate_recvs.at[k], mate),
            remote(
                last.at[at_last], got_last.at[at_last],
                mate_sends.at[chips + k], mate_recvs.at[chips + k], mate,
            ),
        )

    def chip_copies(k):
        at, at_last = group_of(k)
        peer = (chip_at(k) * 2 + core, quad)
        return (
            remote(sum_main.at[at], wide_main.at[k], chip_sends.at[k], chip_recvs.at[k], peer),
            remote(
                sum_last.at[at_last], wide_last.at[k],
                chip_sends.at[chips + k], chip_recvs.at[chips + k], peer,
            ),
        )

    fetch(0, picks_a, 0).start()
    fetch(1, picks_b, 1).start()
    fetch(0, picks_a, 0).wait()
    gather(picks_a, rows_a)
    fetch(2, picks_a, 0).start()
    pl.semaphore_wait(barrier, len(wide_peers) + len(quad_peers))

    def pair(i, carry):
        slot = 2 * i
        fetch(slot + 1, picks_b, 1).wait()
        gather(picks_b, rows_b)
        finish(slot, rows_a)
        fetch(slot + 3, picks_b, 1).start()
        fetch(slot + 2, picks_a, 0).wait()
        gather(picks_a, rows_a)
        finish(slot + 1, rows_b)
        fetch(slot + 4, picks_a, 0).start()
        return carry

    def step(k, carry):
        lax.fori_loop(k * n_quad // 2, (k + 1) * n_quad // 2, pair, 0)

        @pl.when(k < chips)
        def _():
            for copy in mate_copies(k):
                copy.start()

        @pl.when(k >= chips)
        def _():
            own = k - chips
            for copy in mate_copies(own):
                copy.wait_recv()
            at, at_last = group_of(own)
            from_at, from_last = group_of(k)
            sum_main[at] = main[from_at] + got_main[at]
            sum_last[at_last, :] = last[from_last, :] + got_last[at_last, :]

            @pl.when(own < chips - 1)
            def _():
                for copy in chip_copies(own):
                    copy.start()

        return carry

    lax.fori_loop(0, 2 * chips, step, 0)
    fetch(0, picks_a, 0).wait()
    fetch(0, picks_b, 1).wait()
    for k in range(chips):
        for copy in mate_copies(k):
            copy.wait_send()
    for k in range(chips - 1):
        for copy in chip_copies(k):
            copy.wait()

    def add_row(to):
        row = sum_main[(chips - 1) * n_quad + to]
        for k in range(chips - 1):
            row = row + wide_main[k, to]
        row_main[to] = row

    sem_at = [0]

    def send(src, dst, peer):
        sem = sem_at[0]
        sem_at[0] += 1
        copy = remote(src, dst, sends.at[sem], recvs.at[sem], peer)
        copy.start()
        return copy

    ends = sum_last[(chips - 1) * tall :, :]
    for k in range(chips - 1):
        ends = ends + wide_last[k]
    row_last[...] = ends
    copies = []
    for k, peer in enumerate(quad_peers):
        add_row(peer[1])
        copies.append(send(row_main.at[peer[1]], quad_main.at[k], peer))
        copies.append(send(row_last, quad_last.at[k], peer))
    add_row(quad)
    for copy in copies:
        copy.wait()
    total = row_main[quad]
    ends = [row_last[pl.ds(quad * lines + i, 1), :] for i in range(lines)]
    for k in range(n_quad - 1):
        total = total + quad_main[k]
        ends = [e + quad_last[k, pl.ds(quad * lines + i, 1), :] for i, e in enumerate(ends)]
    end = jnp.concatenate(ends, axis=1)
    sketch[:cols, :] = total
    sketch[cols : cols + 1, :] = end

    group = jnp.concatenate([owners[me, i : i + 1] for i in range(lines)], axis=1)
    first = lax.broadcasted_iota(jnp.int32, (8, per_dev), 0) == 0
    right = jnp.concatenate([total, jnp.where(first, end, 0.0)], axis=0)
    left = jnp.concatenate([jnp.where(group == g, total, 0.0) for g in range(GROUPS)], axis=0)
    part = contract_last(right, left, precision=lax.Precision.HIGHEST)
    part = part * (GROUPS / (per_dev * devices))
    span = GROUPS * cols // n_quad
    block = lax.broadcasted_iota(jnp.int32, (8, LANES), 1) // span
    for q in range(n_quad):
        packed = jnp.zeros((8, LANES), jnp.float32)
        for tile in range(part.shape[0] // 8):
            turned = part[tile * 8 : tile * 8 + 8, :]
            if (tile - q) % n_quad:
                turned = pltpu.roll(turned, (tile - q) % n_quad * span, 1)
            packed = jnp.where(block == tile, turned, packed)
        own_gram[q] = packed
    copies = [send(own_gram.at[peer[1]], quad_gram.at[k], peer) for k, peer in enumerate(quad_peers)]
    for copy in copies:
        copy.wait()
    packed = own_gram[quad]
    for k in range(n_quad - 1):
        packed = packed + quad_gram[k]
    wide_gram[0] = packed
    copies = [send(wide_gram.at[0], wide_gram.at[k + 1], peer) for k, peer in enumerate(wide_peers)]
    for copy in copies:
        copy.wait()
    packed = wide_gram[wide]
    for w in range(1, n_wide):
        packed = packed + wide_gram[(wide + n_wide - w) % n_wide]
    gram[...] = packed


def finish_kernel(sketch_in, gram_in, sketch, gram):
    owned, cols, width = gram.shape
    sketch[...] = sketch_in[...]
    turned = gram_in[...].T
    for tile in range(-(-width // 8)):
        columns = min(8, width - tile * 8)
        for g in range(owned):
            at = (tile * owned + g) * cols
            gram[g, :, tile * 8 : tile * 8 + columns] = turned[at : at + cols, :columns]


def shards(n_wide, n_quad, basis, target, sign_bits, samples, owners):
    cols, rows = basis.shape
    devices = n_wide * n_quad
    total_samples = samples.shape[0]
    per_dev = total_samples // devices
    lines = per_dev // LANES
    scale = 1.0 / math.sqrt(rows * devices)
    chunk = rows // HIGH
    mids = chunk // LINE
    vmem = pl.BlockSpec(memory_space=pltpu.VMEM)
    f32 = jnp.float32
    half, chips = devices // 2, n_wide // 2
    flat = (8, LANES)
    spaces = [
        (devices, cols, per_dev), (devices * lines, LANES),
        (half, cols, per_dev), (half * lines, LANES),
        (half, cols, per_dev), (half * lines, LANES),
        (chips - 1, n_quad, cols, per_dev), (chips - 1, n_quad * lines, LANES),
        (n_quad, cols, per_dev), (n_quad * lines, LANES),
        (n_quad - 1, cols, per_dev), (n_quad - 1, n_quad * lines, LANES),
        (n_wide, *flat), (n_quad, *flat), (n_quad - 1, *flat),
    ]
    copies = [2 * chips, 2 * chips, 3 * (n_quad - 1) + n_wide - 1]
    sketch, gram = pl.pallas_call(
        functools.partial(sketch_kernel, n_wide, n_quad, scale),
        out_shape=(
            jax.ShapeDtypeStruct((cols + 1, per_dev), f32),
            jax.ShapeDtypeStruct(flat, f32),
        ),
        in_specs=[
            vmem,
            vmem,
            pl.BlockSpec(memory_space=pl.ANY),
            pl.BlockSpec(memory_space=pl.ANY),
            pl.BlockSpec(memory_space=pl.ANY),
        ],
        out_specs=(vmem, vmem),
        scratch_shapes=[
            pltpu.VMEM((HIGH, chunk // LANES, LANES), jnp.int32),
            pltpu.VMEM((HIGH, cols, chunk), f32),
            pltpu.VMEM((HIGH, chunk // LANES, LANES), f32),
            pltpu.SemaphoreType.DMA((3, HIGH)),
            pltpu.VMEM((mids, HIGH * SLOT, LINE), f32),
            pltpu.VMEM((rows * SLOT // LANES, LANES), f32),
            pltpu.VMEM((LINE, 2 * LINE), jnp.bfloat16),
            pltpu.VMEM((LANES, 2 * LANES), jnp.bfloat16),
            pltpu.VMEM((devices, lines, LANES), jnp.int32),
            pltpu.SMEM((lines, LANES), jnp.int32),
            pltpu.SMEM((lines, LANES), jnp.int32),
            pltpu.VMEM((per_dev, LANES), f32),
            pltpu.VMEM((per_dev, LANES), f32),
            pltpu.SemaphoreType.DMA((2,)),
        ]
        + [pltpu.VMEM(space, f32) for space in spaces]
        + [pltpu.SemaphoreType.DMA((n,)) for n in copies for _ in range(2)],
        compiler_params=pltpu.CompilerParams(
            vmem_limit_bytes=60 * 1024 * 1024, collective_id=0, has_side_effects=True
        ),
    )(
        samples.reshape(devices, lines, LANES),
        owners.reshape(devices, lines, LANES),
        sign_bits.reshape(-1, LANES),
        basis,
        target.reshape(-1, LANES),
    )
    sketch, gram = pl.pallas_call(
        finish_kernel,
        out_shape=(
            jax.ShapeDtypeStruct((cols + 1, per_dev), f32),
            jax.ShapeDtypeStruct((GROUPS // n_quad, cols, cols + 1), f32),
        ),
        in_specs=[vmem, vmem],
        out_specs=(vmem, vmem),
    )(sketch, gram)
    return sketch.T, gram


def solution(mesh):
    placed = (P(None, ("wide", "quad")), P(("wide", "quad")), P(("wide", "quad")), P(), P())
    return jax.shard_map(
        functools.partial(shards, mesh.shape["wide"], mesh.shape["quad"]),
        mesh=mesh,
        in_specs=placed,
        out_specs=(P(("wide", "quad"), None), P("quad", None, None)),
        check_vma=False,
    )
```

profile of v0, /device:TPU:0, one launch (start us, length us, event | category | flops | bytes accessed | tf_op | source)
XLA Modules:
  0.0 40.5 jit_solution(12676602989429076532)
XLA Ops:
  0.6 38.4 %shard_map.68 = (f32[17,256]{1,0:T(8,128)}, f32[8,128]{1,0:T(8,128)}) custom-call(s32[32,2,128]{2,1,0:T(2,128)} %bitcast.7, s32[32,2,128]{2,1,0:T(2,128)} %bitcast.8, s32[512,128]{1,0:T(8,128)} %bitcast.5, f32[16,65536]{1,0:T(8,128)} %x_in.1, f32[512,128]{1,0:T(8,128)} %bitcast.6), custom_call_target="tpu_custom_call" | custom-call | tf_op jit(solution)/shard_map/pallas_call | solution.py:369
  39.0 1.5 %shard_map.69 = (f32[17,256]{1,0:T(8,128)}, f32[2,16,17]{2,1,0:T(8,128)}) custom-call(f32[17,256]{1,0:T(8,128)} %get-tuple-element.6.sketch_in, f32[8,128]{1,0:T(8,128)} %get-tuple-element.7.gram_in), custom_call_target="tpu_custom_call" | custom-call | tf_op jit(solution)/shard_map/pallas_call | solution.py:411
where the time goes:
time: 40.7 us; the launch traced here: 40.5 us
  Pallas kernels  39.9 us (98%)
  between operations  0.64 us (2%)
    pallas_call x1, Pallas kernels, shards(): pl.pallas_call(functools.partial(sketch_kernel, n_wide, n_quad, scale), o...  38.4 us
    pallas_call x1, Pallas kernels, shards(): pl.pallas_call(finish_kernel, out_shape=(jax.ShapeDtypeStruct((cols + 1,...  1.51 us

commit v1 on v0

--- a/solution.py
+++ b/solution.py
@@ -52,9 +52,9 @@
 
 
 def sketch_kernel(
-    n_wide, n_quad, scale, samp, owners, bits_in, x_in, t_in, sketch, gram,
+    n_wide, n_quad, scale, samp_in, owners_in, bits_in, x_in, t_in, sketch, gram,
     bits_all, x_all, t_all, load_sems,
-    field, table, walsh, unit, picks, picks_a, picks_b, rows_a, rows_b, sems,
+    field, table, walsh, unit, samp, owners, picks, slots_all, rows_a, rows_b, sems,
     main, last, got_main, got_last, sum_main, sum_last, wide_main, wide_last,
     row_main, row_last, quad_main, quad_last, wide_gram, own_gram, quad_gram,
     mate_sends, mate_recvs, chip_sends, chip_recvs, sends, recvs
@@ -83,9 +83,13 @@
             pltpu.make_async_copy(x_in.at[:, pl.ds(at, chunk)], x_all.at[h], load_sems.at[2, h]),
         )
 
+    samp_copy = pltpu.make_async_copy(samp_in, samp, sems.at[0])
+    owners_copy = pltpu.make_async_copy(owners_in, owners, sems.at[1])
+    samp_copy.start()
     for h in range(HIGH):
         for copy in loads(h):
             copy.start()
+    owners_copy.start()
     for peer in wide_peers + quad_peers:
         pl.semaphore_signal(barrier, inc=1, device_id=peer, device_id_type=MESH)
     a = lax.broadcasted_iota(jnp.int32, (LINE, LINE), 0)
@@ -98,7 +102,10 @@
     line = jnp.where(a == b, 1.0, 0.0).astype(jnp.bfloat16)
     unit[:, :LANES] = line
     unit[:, LANES:] = line
+    samp_copy.wait()
     picks[...] = samp[...] & (table.shape[0] - 1)
+    picks_copy = pltpu.make_async_copy(picks, slots_all, sems.at[2])
+    picks_copy.start()
 
     row = lax.broadcasted_iota(jnp.int32, (8, LANES), 0)
 
@@ -155,13 +162,10 @@
         to_wide = chip_at(slot // n_quad % chips) * 2 + to_core
         return to_wide * n_quad + slot % n_quad
 
-    def fetch(slot, slots, sem):
-        slot = jnp.minimum(slot, devices - 1)
-        return pltpu.make_async_copy(picks.at[device_at(slot)], slots, sems.at[sem])
-
-    def gather(slots, rows):
+    def gather(slot, rows):
+        dev = device_at(jnp.minimum(slot, devices - 1))
         for r in range(per_dev):
-            rows[r : r + 1, :] = table[pl.ds(slots[r // LANES, r % LANES], 1), :]
+            rows[r : r + 1, :] = table[pl.ds(slots_all[dev, r // LANES, r % LANES], 1), :]
 
     def finish(slot, rows):
         dev = device_at(slot)
@@ -210,23 +214,17 @@
             ),
         )
 
-    fetch(0, picks_a, 0).start()
-    fetch(1, picks_b, 1).start()
-    fetch(0, picks_a, 0).wait()
-    gather(picks_a, rows_a)
-    fetch(2, picks_a, 0).start()
+    picks_copy.wait()
+    owners_copy.wait()
+    gather(0, rows_a)
     pl.semaphore_wait(barrier, len(wide_peers) + len(quad_peers))
 
     def pair(i, carry):
         slot = 2 * i
-        fetch(slot + 1, picks_b, 1).wait()
-        gather(picks_b, rows_b)
+        gather(slot + 1, rows_b)
         finish(slot, rows_a)
-        fetch(slot + 3, picks_b, 1).start()
-        fetch(slot + 2, picks_a, 0).wait()
-        gather(picks_a, rows_a)
+        gather(slot + 2, rows_a)
         finish(slot + 1, rows_b)
-        fetch(slot + 4, picks_a, 0).start()
         return carry
 
     def step(k, carry):
@@ -255,8 +253,6 @@
         return carry
 
     lax.fori_loop(0, 2 * chips, step, 0)
-    fetch(0, picks_a, 0).wait()
-    fetch(0, picks_b, 1).wait()
     for k in range(chips):
         for copy in mate_copies(k):
             copy.wait_send()
@@ -373,8 +369,8 @@
             jax.ShapeDtypeStruct(flat, f32),
         ),
         in_specs=[
-            vmem,
-            vmem,
+            pl.BlockSpec(memory_space=pl.ANY),
+            pl.BlockSpec(memory_space=pl.ANY),
             pl.BlockSpec(memory_space=pl.ANY),
             pl.BlockSpec(memory_space=pl.ANY),
             pl.BlockSpec(memory_space=pl.ANY),
@@ -390,11 +386,12 @@
             pltpu.VMEM((LINE, 2 * LINE), jnp.bfloat16),
             pltpu.VMEM((LANES, 2 * LANES), jnp.bfloat16),
             pltpu.VMEM((devices, lines, LANES), jnp.int32),
-            pltpu.SMEM((lines, LANES), jnp.int32),
-            pltpu.SMEM((lines, LANES), jnp.int32),
+            pltpu.VMEM((devices, lines, LANES), jnp.int32),
+            pltpu.VMEM((devices, lines, LANES), jnp.int32),
+            pltpu.SMEM((devices, lines, LANES), jnp.int32),
             pltpu.VMEM((per_dev, LANES), f32),
             pltpu.VMEM((per_dev, LANES), f32),
-            pltpu.SemaphoreType.DMA((2,)),
+            pltpu.SemaphoreType.DMA((3,)),
         ]
         + [pltpu.VMEM(space, f32) for space in spaces]
         + [pltpu.SemaphoreType.DMA((n,)) for n in copies for _ in range(2)],

time: 40.7 us -> 38.2 us (0.939)
  Pallas kernels: 39.9 us -> 37.4 us
    pallas_call x1, Pallas kernels: 38.4 us -> 35.9 us  [shards(): pl.pallas_call(functools.partial(sketch_kernel, n_wide, n_quad, scale), o...]
where the time goes in v1:
time: 38.2 us; the launch traced here: 38.1 us
  Pallas kernels  37.4 us (98%)
  between operations  0.64 us (2%)
    pallas_call x1, Pallas kernels, shards(): pl.pallas_call(functools.partial(sketch_kernel, n_wide, n_quad, scale), o...  35.9 us
    pallas_call x1, Pallas kernels, shards(): pl.pallas_call(finish_kernel, out_shape=(jax.ShapeDtypeStruct((cols + 1,...  1.51 us

profile of v1, /device:TPU:0, one launch (start us, length us, event | category | flops | bytes accessed | tf_op | source)
XLA Modules:
  0.0 38.1 jit_solution(11089885698856585185)
XLA Ops:
  0.6 35.9 %shard_map.68 = (f32[17,256]{1,0:T(8,128)}, f32[8,128]{1,0:T(8,128)}) custom-call(s32[32,2,128]{2,1,0:T(2,128)} %bitcast.7, s32[32,2,128]{2,1,0:T(2,128)} %bitcast.8, s32[512,128]{1,0:T(8,128)} %bitcast.5, f32[16,65536]{1,0:T(8,128)} %x_in.1, f32[512,128]{1,0:T(8,128)} %bitcast.6), custom_call_target="tpu_custom_call" | custom-call | tf_op jit(solution)/shard_map/pallas_call | solution.py:365
  36.5 1.5 %shard_map.69 = (f32[17,256]{1,0:T(8,128)}, f32[2,16,17]{2,1,0:T(8,128)}) custom-call(f32[17,256]{1,0:T(8,128)} %get-tuple-element.6.sketch_in, f32[8,128]{1,0:T(8,128)} %get-tuple-element.7.gram_in), custom_call_target="tpu_custom_call" | custom-call | tf_op jit(solution)/shard_map/pallas_call | solution.py:408

commit v2 on v1

v2 whole, which is shorter than its diff:
```python
import functools
import math

import jax
import jax.numpy as jnp
from jax import lax
from jax.experimental import pallas as pl
from jax.experimental.pallas import tpu as pltpu
from jax.sharding import PartitionSpec as P

GROUPS = 8
LANES = 128
LINE = 256
HIGH = 8
MESH = pl.DeviceIdType.MESH


def bits_of(n):
    return n.bit_length() - 1


def parity(x, nbits):
    shift = 1
    while shift < nbits:
        x = x ^ (x >> shift)
        shift *= 2
    return x & 1


def butterfly(parts):
    half = 1
    while half < len(parts):
        for at in range(0, len(parts), 2 * half):
            for i in range(at, at + half):
                parts[i], parts[i + half] = parts[i] + parts[i + half], parts[i] - parts[i + half]
        half *= 2
    return parts


def split(x):
    top = x.astype(jnp.bfloat16)
    return top, (x - top.astype(jnp.float32)).astype(jnp.bfloat16)


def contract_last(a, b, **kw):
    return lax.dot_general(a, b, (((1,), (1,)), ((), ())), preferred_element_type=jnp.float32, **kw)


def sketch_kernel(
    n_wide, n_quad, scale, samp_in, owners_in, bits_in, x_in, t_in, sketch, gram,
    bits_all, x_all, t_all, load_sems, flips,
    field, spare, table, walsh, unit, samp, owners, picks, slot_of, sign_of, slots, rows_of, sems, pick_sems,
    mine, got, sums, wide_in, row, quad_in, wide_gram, own_gram, quad_gram,
    mate_sends, mate_recvs, chip_sends, chip_recvs, sends, recvs
):
    chunk = x_all.shape[2]
    lines_in = chunk // LANES
    parts = LINE // LANES
    mids = chunk // LINE
    local_bits = bits_of(HIGH * chunk)
    cols = x_all.shape[1]
    devices = n_wide * n_quad
    lines = samp.shape[0] // devices
    per_dev = lines * LANES
    kept = LANES // (cols + 1)
    ends_at = kept * cols
    spill_blocks = -(-mids // kept)
    wide = lax.axis_index("wide")
    quad = lax.axis_index("quad")
    me = wide * n_quad + quad
    core, chip, chips = wide % 2, wide // 2, n_wide // 2
    mate = (wide + 1 - 2 * core, quad)
    wide_peers = [((wide + k) % n_wide, quad) for k in range(1, n_wide)]
    quad_peers = [(wide, (quad + k) % n_quad) for k in range(1, n_quad)]
    barrier = pltpu.get_barrier_semaphore()

    def loads(h):
        at = pl.multiple_of(h * chunk, chunk)
        rows = pl.ds(pl.multiple_of(h * lines_in, lines_in), lines_in)
        return (
            pltpu.make_async_copy(bits_in.at[rows], bits_all.at[rows], load_sems.at[0, h]),
            pltpu.make_async_copy(t_in.at[rows], t_all.at[rows], load_sems.at[1, h]),
            pltpu.make_async_copy(x_in.at[:, pl.ds(at, chunk)], x_all.at[h], load_sems.at[2, h]),
        )

    samp_copy = pltpu.make_async_copy(samp_in, samp, sems.at[0])
    owners_copy = pltpu.make_async_copy(owners_in, owners, sems.at[1])
    samp_copy.start()
    for h in range(HIGH):
        for copy in loads(h):
            copy.start()
    owners_copy.start()
    for peer in wide_peers + quad_peers:
        pl.semaphore_signal(barrier, inc=1, device_id=peer, device_id_type=MESH)
    a = lax.broadcasted_iota(jnp.int32, (LINE, LINE), 0)
    b = lax.broadcasted_iota(jnp.int32, (LINE, LINE), 1)
    line = (1 - 2 * parity(a & b, bits_of(LINE))).astype(jnp.float32).astype(jnp.bfloat16)
    walsh[:, :LINE] = line
    walsh[:, LINE:] = line
    a = lax.broadcasted_iota(jnp.int32, (LANES, LANES), 0)
    b = lax.broadcasted_iota(jnp.int32, (LANES, LANES), 1)
    line = jnp.where(a == b, 1.0, 0.0).astype(jnp.bfloat16)
    unit[:, :LANES] = line
    unit[:, LANES:] = line
    pad = t_all.shape[0] - HIGH * lines_in
    t_all[HIGH * lines_in :, :] = jnp.zeros((pad, LANES), jnp.float32)

    samp_copy.wait()
    number = samp[...]
    mid_of = (number >> bits_of(LINE)) & (mids - 1)
    high_of = (number >> bits_of(chunk)) & (HIGH - 1)
    block = jnp.zeros_like(mid_of)
    for i in range(1, spill_blocks):
        block = block + jnp.where(mid_of >= i * kept, 1, 0)
    spilled = high_of >= kept
    picks[...] = jnp.where(spilled, mids + block, mid_of) * LINE + (number & (LINE - 1))
    slot_of[...] = jnp.where(spilled, mid_of - kept * block, high_of)
    sign = parity((number >> local_bits) & me, bits_of(devices))
    sign_of[...] = (1 - 2 * sign).astype(jnp.float32) * scale

    def chip_at(k):
        return (chip + 1 + k) & (chips - 1)

    def base_of(group, own):
        to_core = (core + 1 + own) & 1
        return (chip_at(group) * 2 + to_core) * n_quad

    def even_base(turn):
        group = jnp.minimum(jnp.maximum(turn - 1, 0), chips - 1)
        return base_of(group, jnp.minimum(turn, 1))

    def odd_base(turn):
        return base_of(jnp.minimum(turn + 1, chips - 1), (turn + 1) >> bits_of(chips))

    def fetch(dev, buf):
        at = pl.ds(dev * lines, lines)
        return pltpu.make_async_copy(picks.at[at], slots.at[buf], pick_sems.at[buf])

    def fetch_even(turn):
        base, after = even_base(turn), odd_base(turn)
        return [fetch(base + j if j < n_quad else after, j - 1) for j in range(1, n_quad + 1)]

    def fetch_odd(turn):
        base, after = odd_base(turn), even_base(turn + 1)
        return [fetch(base + j if j < n_quad else after, n_quad + j - 1) for j in range(1, n_quad + 1)]

    first_fetch = fetch(even_base(0), 2 * n_quad)
    for copy in [first_fetch] + fetch_even(0) + fetch_odd(0):
        copy.start()

    low = lax.broadcasted_iota(jnp.int32, (8, LANES), 0)
    signs = [1.0 - 2.0 * ((low >> i) & 1).astype(jnp.float32) for i in range(3)]

    def across(x, i):
        step = 1 << i
        down = pltpu.roll(x, step, 0)
        if step == 4:
            return x * signs[i] + down
        return x * signs[i] + jnp.where(signs[i] < 0, down, pltpu.roll(x, 8 - step, 0))

    def first_pass(high, carry):
        for copy in loads(high):
            copy.wait()
        rows = pl.ds(pl.multiple_of(high * lines_in, lines_in), lines_in)
        flip = (1 - 2 * bits_all[rows]).astype(jnp.float32)
        flips[...] = flip
        t = t_all[rows] * flip
        t = butterfly([t[i * 8 : i * 8 + 8] for i in range(lines_in // 8)])
        for i in range(bits_of(parts), 3):
            t = [across(x, i) for x in t]
        for i, value in enumerate(t):
            t_all[pl.ds(pl.multiple_of(high * lines_in + i * 8, 8), 8), :] = value
        x = x_all.at[high]
        at = pl.multiple_of(high * cols, cols)
        for part in range(parts):
            for tile in range(cols // 8):
                values = []
                for mid in range(mids):
                    line = mid * parts + part
                    flip = flips[pl.ds(line, 8, stride=0), :]
                    values.append(x[tile * 8 : tile * 8 + 8, line * LANES : (line + 1) * LANES] * flip)
                for mid, value in enumerate(butterfly(values)):
                    field[mid, pl.ds(at + tile * 8, 8), part * LANES : (part + 1) * LANES] = value
        return carry

    lax.fori_loop(0, HIGH, first_pass, 0)
    for i in range(lines_in // 8):
        t = butterfly([t_all[h * lines_in + i * 8 : h * lines_in + i * 8 + 8, :] for h in range(HIGH)])
        for h, value in enumerate(t):
            t_all[h * lines_in + i * 8 : h * lines_in + i * 8 + 8, :] = value
    blank = jnp.zeros((LANES - ends_at - 8, LANES), jnp.float32)

    def change(blocks, at):
        both = jnp.concatenate(split(jnp.concatenate(blocks, axis=0)), axis=1)
        out = contract_last(walsh[...], both)
        for i in range(len(blocks)):
            table[pl.ds(at + i * LINE, LINE), :] = out[:, i * LANES : (i + 1) * LANES]

    def mix(pair, carry):
        blocks = []
        for i in range(2):
            mid = 2 * pair + i
            halves = []
            for part in range(parts):
                across_lanes = slice(part * LANES, (part + 1) * LANES)
                values = [
                    butterfly([field[mid, h * cols + r : h * cols + r + 8, across_lanes] for h in range(HIGH)])
                    for r in range(0, cols, 8)
                ]
                for r, value in enumerate(values):
                    spare[mid, r * 8 : r * 8 + 8, across_lanes] = value[kept]
                t = t_all[pl.ds(mid * parts + part, 8, stride=lines_in), :]
                mains = [value[h] for h in range(kept) for value in values]
                halves.append(jnp.concatenate(mains + [t, blank], axis=0))
            blocks.append(jnp.concatenate(halves, axis=1))
        change(blocks, pl.multiple_of(pair * 2 * LINE, 2 * LINE))
        return carry

    lax.fori_loop(0, mids // 2, mix, 0, unroll=4)
    for first in range(0, spill_blocks, 2):
        blocks = []
        for i in range(first, min(first + 2, spill_blocks)):
            halves = []
            for part in range(parts):
                across_lanes = slice(part * LANES, (part + 1) * LANES)
                mains = [
                    spare[mid, :, across_lanes] if mid < mids else jnp.zeros((cols, LANES), jnp.float32)
                    for mid in range(i * kept, (i + 1) * kept)
                ]
                t = t_all[pl.ds(kept * lines_in + i * kept * parts + part, 8, stride=parts), :]
                halves.append(jnp.concatenate(mains + [t, blank], axis=0))
            blocks.append(jnp.concatenate(halves, axis=1))
        change(blocks, (mids + first) * LINE)

    def gather(buf, at):
        for r in range(per_dev):
            rows_of[at, r : r + 1, :] = table[pl.ds(slots[buf, r // LANES, r % LANES], 1), :]

    def finish(slot, dev, at):
        out = contract_last(unit[...], jnp.concatenate(split(rows_of[at]), axis=1))
        for i in range(lines):
            group = slot_of[pl.ds(dev * lines + i, 8, stride=0), :]
            sign = sign_of[pl.ds(dev * lines + i, 8, stride=0), :]
            half = out[:, i * LANES : (i + 1) * LANES]
            for r in range(0, cols, 8):
                total = half[r : r + 8]
                for g in range(1, kept):
                    total = jnp.where(group == g, half[g * cols + r : g * cols + r + 8], total)
                mine[slot, i * cols + r : i * cols + r + 8, :] = total * sign
            end = jnp.where(low == group, half[ends_at : ends_at + 8], 0.0)
            end = jnp.sum(end, axis=0, keepdims=True) * sign[:1]
            mine[slot, lines * cols + i : lines * cols + i + 1, :] = end

    def remote(src, dst, send_sem, recv_sem, peer):
        return pltpu.make_async_remote_copy(
            src_ref=src, dst_ref=dst, send_sem=send_sem, recv_sem=recv_sem,
            device_id=peer, device_id_type=MESH,
        )

    def group_of(k):
        return pl.ds(k * n_quad, n_quad)

    def mate_copy(k):
        at = group_of(k)
        return remote(mine.at[at], got.at[at], mate_sends.at[k], mate_recvs.at[k], mate)

    def chip_copy(k):
        peer = (chip_at(k) * 2 + core, quad)
        return remote(sums.at[group_of(k)], wide_in.at[k], chip_sends.at[k], chip_recvs.at[k], peer)

    def own_sum(group):
        mate_copy(group).wait_recv()
        at = group_of(group)
        sums[at] = mine[group_of(chips + group)] + got[at]

    first_fetch.wait()
    gather(2 * n_quad, 0)
    pl.semaphore_wait(barrier, len(wide_peers) + len(quad_peers))
    owners_copy.wait()

    def work(base, slot, buf, count):
        for j in range(n_quad):
            if j < count:
                gather(buf + j, (j + 1) % n_quad)
            finish(slot + j, base + j, j)

    def turns(turn, carry):
        for copy in fetch_even(turn):
            copy.wait()
        own = jnp.minimum(turn, 1)
        group = jnp.maximum(turn - 1, 0)
        work(even_base(turn), (own * chips + group) * n_quad, 0, n_quad)

        @pl.when(turn == 0)
        def _():
            mate_copy(0).start()

        @pl.when(turn > 0)
        def _():
            own_sum(turn - 1)
            chip_copy(turn - 1).start()

        @pl.when(turn < chips - 1)
        def _():
            for copy in fetch_even(turn + 1):
                copy.start()

        for copy in fetch_odd(turn):
            copy.wait()

        @pl.when(turn < chips - 1)
        def _():
            work(odd_base(turn), (turn + 1) * n_quad, n_quad, n_quad)
            mate_copy(turn + 1).start()
            for copy in fetch_odd(turn + 1):
                copy.start()

        @pl.when(turn == chips - 1)
        def _():
            work(odd_base(turn), (2 * chips - 1) * n_quad, n_quad, n_quad - 1)
            own_sum(chips - 1)

        return carry

    lax.fori_loop(0, chips, turns, 0)
    for k in range(chips):
        mate_copy(k).wait_send()
    for k in range(chips - 1):
        chip_copy(k).wait()

    def add_row(to):
        total = sums[(chips - 1) * n_quad + to]
        for k in range(chips - 1):
            total = total + wide_in[k, to]
        row[to] = total

    sem_at = [0]

    def send(src, dst, peer):
        sem = sem_at[0]
        sem_at[0] += 1
        copy = remote(src, dst, sends.at[sem], recvs.at[sem], peer)
        copy.start()
        return copy

    copies = []
    for k, peer in enumerate(quad_peers):
        add_row(peer[1])
        copies.append(send(row.at[peer[1]], quad_in.at[k], peer))
    add_row(quad)
    for copy in copies:
        copy.wait()
    total = row[quad]
    for k in range(n_quad - 1):
        total = total + quad_in[k]
    end = jnp.concatenate([total[lines * cols + i : lines * cols + i + 1] for i in range(lines)], axis=1)
    total = jnp.concatenate([total[i * cols : (i + 1) * cols] for i in range(lines)], axis=1)
    sketch[:cols, :] = total
    sketch[cols : cols + 1, :] = end

    group = jnp.concatenate([owners[pl.ds(me * lines + i, cols, stride=0), :] for i in range(lines)], axis=1)
    first = lax.broadcasted_iota(jnp.int32, (8, per_dev), 0) == 0
    right = jnp.concatenate([total, jnp.where(first, end, 0.0)], axis=0)
    left = jnp.concatenate([jnp.where(group == g, total, 0.0) for g in range(GROUPS)], axis=0)
    part = contract_last(right, left, precision=lax.Precision.HIGHEST)
    part = part * (GROUPS / (per_dev * devices))
    span = GROUPS * cols // n_quad
    block = lax.broadcasted_iota(jnp.int32, (8, LANES), 1) // span
    for q in range(n_quad):
        packed = jnp.zeros((8, LANES), jnp.float32)
        for tile in range(part.shape[0] // 8):
            turned = part[tile * 8 : tile * 8 + 8, :]
            if (tile - q) % n_quad:
                turned = pltpu.roll(turned, (tile - q) % n_quad * span, 1)
            packed = jnp.where(block == tile, turned, packed)
        own_gram[q] = packed
    copies = [send(own_gram.at[peer[1]], quad_gram.at[k], peer) for k, peer in enumerate(quad_peers)]
    for copy in copies:
        copy.wait()
    packed = own_gram[quad]
    for k in range(n_quad - 1):
        packed = packed + quad_gram[k]
    wide_gram[0] = packed
    copies = [send(wide_gram.at[0], wide_gram.at[k + 1], peer) for k, peer in enumerate(wide_peers)]
    for copy in copies:
        copy.wait()
    packed = wide_gram[wide]
    for w in range(1, n_wide):
        packed = packed + wide_gram[(wide + n_wide - w) % n_wide]
    gram[...] = packed


def finish_kernel(sketch_in, gram_in, sketch, gram):
    owned, cols, width = gram.shape
    sketch[...] = sketch_in[...]
    turned = gram_in[...].T
    for tile in range(-(-width // 8)):
        columns = min(8, width - tile * 8)
        for g in range(owned):
            at = (tile * owned + g) * cols
            gram[g, :, tile * 8 : tile * 8 + columns] = turned[at : at + cols, :columns]


def shards(n_wide, n_quad, basis, target, sign_bits, samples, owners):
    cols, rows = basis.shape
    devices = n_wide * n_quad
    total_samples = samples.shape[0]
    per_dev = total_samples // devices
    lines = per_dev // LANES
    scale = 1.0 / math.sqrt(rows * devices)
    chunk = rows // HIGH
    mids = chunk // LINE
    vmem = pl.BlockSpec(memory_space=pltpu.VMEM)
    f32 = jnp.float32
    half, chips = devices // 2, n_wide // 2
    flat = (8, LANES)
    packed = (lines * (cols + 1), LANES)
    kept = LANES // (cols + 1)
    blocks = mids + -(-mids // kept)
    spaces = [
        (devices, *packed), (half, *packed), (half, *packed), (chips - 1, n_quad, *packed),
        (n_quad, *packed), (n_quad - 1, *packed),
        (n_wide, *flat), (n_quad, *flat), (n_quad - 1, *flat),
    ]
    copies = [chips, chips - 1, 2 * (n_quad - 1) + n_wide - 1]
    sketch, gram = pl.pallas_call(
        functools.partial(sketch_kernel, n_wide, n_quad, scale),
        out_shape=(
            jax.ShapeDtypeStruct((cols + 1, per_dev), f32),
            jax.ShapeDtypeStruct(flat, f32),
        ),
        in_specs=[
            pl.BlockSpec(memory_space=pl.ANY),
            pl.BlockSpec(memory_space=pl.ANY),
            pl.BlockSpec(memory_space=pl.ANY),
            pl.BlockSpec(memory_space=pl.ANY),
            pl.BlockSpec(memory_space=pl.ANY),
        ],
        out_specs=(vmem, vmem),
        scratch_shapes=[
            pltpu.VMEM((rows // LANES, LANES), jnp.int32),
            pltpu.VMEM((HIGH, cols, chunk), f32),
            pltpu.VMEM((rows // LANES + 2 * 8, LANES), f32),
            pltpu.SemaphoreType.DMA((3, HIGH)),
            pltpu.VMEM((chunk // LANES, LANES), f32),
            pltpu.VMEM((mids, HIGH * cols, LINE), f32),
            pltpu.VMEM((mids, cols, LINE), f32),
            pltpu.VMEM((blocks * LINE, LANES), f32),
            pltpu.VMEM((LINE, 2 * LINE), jnp.bfloat16),
            pltpu.VMEM((LANES, 2 * LANES), jnp.bfloat16),
            pltpu.VMEM((devices * lines, LANES), jnp.int32),
            pltpu.VMEM((devices * lines, LANES), jnp.int32),
            pltpu.VMEM((devices * lines, LANES), jnp.int32),
            pltpu.VMEM((devices * lines, LANES), jnp.int32),
            pltpu.VMEM((devices * lines, LANES), f32),
            pltpu.SMEM((2 * n_quad + 1, lines, LANES), jnp.int32),
            pltpu.VMEM((n_quad, per_dev, LANES), f32),
            pltpu.SemaphoreType.DMA((2,)),
            pltpu.SemaphoreType.DMA((2 * n_quad + 1,)),
        ]
        + [pltpu.VMEM(space, f32) for space in spaces]
        + [pltpu.SemaphoreType.DMA((n,)) for n in copies for _ in range(2)],
        compiler_params=pltpu.CompilerParams(
            vmem_limit_bytes=60 * 1024 * 1024, collective_id=0, has_side_effects=True
        ),
    )(
        samples.reshape(-1, LANES),
        owners.reshape(-1, LANES),
        sign_bits.reshape(-1, LANES),
        basis,
        target.reshape(-1, LANES),
    )
    sketch, gram = pl.pallas_call(
        finish_kernel,
        out_shape=(
            jax.ShapeDtypeStruct((cols + 1, per_dev), f32),
            jax.ShapeDtypeStruct((GROUPS // n_quad, cols, cols + 1), f32),
        ),
        in_specs=[vmem, vmem],
        out_specs=(vmem, vmem),
    )(sketch, gram)
    return sketch.T, gram


def solution(mesh):
    placed = (P(None, ("wide", "quad")), P(("wide", "quad")), P(("wide", "quad")), P(), P())
    return jax.shard_map(
        functools.partial(shards, mesh.shape["wide"], mesh.shape["quad"]),
        mesh=mesh,
        in_specs=placed,
        out_specs=(P(("wide", "quad"), None), P("quad", None, None)),
        check_vma=False,
    )
```

time: 38.2 us -> 33.1 us (0.87)
  Pallas kernels: 37.4 us -> 32.3 us
    pallas_call x1, Pallas kernels: 35.9 us -> 30.8 us  [shards(): pl.pallas_call(functools.partial(sketch_kernel, n_wide, n_quad, scale), o...]
where the time goes in v2:
time: 33.1 us; the launch traced here: 32.9 us
  Pallas kernels  32.3 us (98%)
  between operations  0.64 us (2%)
    pallas_call x1, Pallas kernels, shards(): pl.pallas_call(functools.partial(sketch_kernel, n_wide, n_quad, scale), o...  30.8 us
    pallas_call x1, Pallas kernels, shards(): pl.pallas_call(finish_kernel, out_shape=(jax.ShapeDtypeStruct((cols + 1,...  1.51 us

profile of v2, /device:TPU:0, one launch (start us, length us, event | category | flops | bytes accessed | tf_op | source)
XLA Modules:
  0.0 32.9 jit_solution(3141814040528213792)
XLA Ops:
  0.6 30.8 %shard_map.68 = (f32[17,256]{1,0:T(8,128)}, f32[8,128]{1,0:T(8,128)}) custom-call(s32[64,128]{1,0:T(8,128)} %bitcast.7, s32[64,128]{1,0:T(8,128)} %bitcast.8, s32[512,128]{1,0:T(8,128)} %bitcast.5, f32[16,65536]{1,0:T(8,128)} %x_in.1, f32[512,128]{1,0:T(8,128)} %bitcast.6), custom_call_target="tpu_custom_call" | custom-call | tf_op jit(solution)/shard_map/pallas_call | solution.py:426
  31.4 1.5 %shard_map.69 = (f32[17,256]{1,0:T(8,128)}, f32[2,16,17]{2,1,0:T(8,128)}) custom-call(f32[17,256]{1,0:T(8,128)} %get-tuple-element.6.sketch_in, f32[8,128]{1,0:T(8,128)} %get-tuple-element.7.gram_in), custom_call_target="tpu_custom_call" | custom-call | tf_op jit(solution)/shard_map/pallas_call | solution.py:473

commit v3 on v2

--- a/solution.py
+++ b/solution.py
@@ -50,8 +50,8 @@
     n_wide, n_quad, scale, samp_in, owners_in, bits_in, x_in, t_in, sketch, gram,
     bits_all, x_all, t_all, load_sems, flips,
     field, spare, table, walsh, unit, samp, owners, picks, slot_of, sign_of, slots, rows_of, sems, pick_sems,
-    mine, got, sums, wide_in, row, quad_in, wide_gram, own_gram, quad_gram,
-    mate_sends, mate_recvs, chip_sends, chip_recvs, sends, recvs
+    mine, got, sums, wide_in, direct_in, row, quad_in, own_gram, mate_gram, pair_gram, gram_in,
+    mate_sends, mate_recvs, chip_sends, chip_recvs, direct_sends, direct_recvs, sends, recvs
 ):
     chunk = x_all.shape[2]
     lines_in = chunk // LANES
@@ -70,8 +70,11 @@
     me = wide * n_quad + quad
     core, chip, chips = wide % 2, wide // 2, n_wide // 2
     mate = (wide + 1 - 2 * core, quad)
-    wide_peers = [((wide + k) % n_wide, quad) for k in range(1, n_wide)]
-    quad_peers = [(wide, (quad + k) % n_quad) for k in range(1, n_quad)]
+    peers = [
+        (((chip + i) & (chips - 1)) * 2 + core, (quad + k) & (n_quad - 1))
+        for i in range(chips) for k in range(n_quad)
+    ]
+    quad_peers = peers[1:n_quad]
     barrier = pltpu.get_barrier_semaphore()
 
     def loads(h):
@@ -90,7 +93,7 @@
         for copy in loads(h):
             copy.start()
     owners_copy.start()
-    for peer in wide_peers + quad_peers:
+    for peer in peers[1:] + [mate]:
         pl.semaphore_signal(barrier, inc=1, device_id=peer, device_id_type=MESH)
     a = lax.broadcasted_iota(jnp.int32, (LINE, LINE), 0)
     b = lax.broadcasted_iota(jnp.int32, (LINE, LINE), 1)
@@ -125,12 +128,19 @@
         to_core = (core + 1 + own) & 1
         return (chip_at(group) * 2 + to_core) * n_quad
 
+    def even_of(turn):
+        inner = (turn > 0) & (turn < chips - 1)
+        return jnp.where(inner, turn - 1, jnp.minimum(turn, chips - 1)), jnp.where(inner, 1, 0)
+
+    def odd_of(turn):
+        own = turn >= chips - 2
+        return jnp.where(own, turn, turn + 1), jnp.where(own, 1, 0)
+
     def even_base(turn):
-        group = jnp.minimum(jnp.maximum(turn - 1, 0), chips - 1)
-        return base_of(group, jnp.minimum(turn, 1))
+        return base_of(*even_of(turn))
 
     def odd_base(turn):
-        return base_of(jnp.minimum(turn + 1, chips - 1), (turn + 1) >> bits_of(chips))
+        return base_of(*odd_of(turn))
 
     def fetch(dev, buf):
         at = pl.ds(dev * lines, lines)
@@ -268,6 +278,22 @@
         peer = (chip_at(k) * 2 + core, quad)
         return remote(sums.at[group_of(k)], wide_in.at[k], chip_sends.at[k], chip_recvs.at[k], peer)
 
+    def direct_copies():
+        far = chips - 2
+        return [
+            remote(
+                sums.at[far * n_quad + k], direct_in.at[quad], direct_sends.at[k], direct_recvs.at[quad],
+                (chip_at(far) * 2 + core, k),
+            )
+            for k in range(n_quad)
+        ]
+
+    def direct_arrivals():
+        return [
+            remote(sums.at[0], direct_in.at[k], direct_sends.at[k], direct_recvs.at[k], peers[n_quad])
+            for k in range(n_quad)
+        ]
+
     def own_sum(group):
         mate_copy(group).wait_recv()
         at = group_of(group)
@@ -275,10 +301,12 @@
 
     first_fetch.wait()
     gather(2 * n_quad, 0)
-    pl.semaphore_wait(barrier, len(wide_peers) + len(quad_peers))
+    pl.semaphore_wait(barrier, len(peers))
     owners_copy.wait()
 
-    def work(base, slot, buf, count):
+    def work(step, base, buf, count):
+        group, own = step
+        slot = (own * chips + group) * n_quad
         for j in range(n_quad):
             if j < count:
                 gather(buf + j, (j + 1) % n_quad)
@@ -287,18 +315,20 @@
     def turns(turn, carry):
         for copy in fetch_even(turn):
             copy.wait()
-        own = jnp.minimum(turn, 1)
-        group = jnp.maximum(turn - 1, 0)
-        work(even_base(turn), (own * chips + group) * n_quad, 0, n_quad)
+        work(even_of(turn), even_base(turn), 0, n_quad)
 
         @pl.when(turn == 0)
         def _():
             mate_copy(0).start()
 
-        @pl.when(turn > 0)
+        @pl.when((turn > 0) & (turn < chips - 1))
         def _():
             own_sum(turn - 1)
             chip_copy(turn - 1).start()
+
+        @pl.when(turn == chips - 1)
+        def _():
+            mate_copy(chips - 1).start()
 
         @pl.when(turn < chips - 1)
         def _():
@@ -310,27 +340,35 @@
 
         @pl.when(turn < chips - 1)
         def _():
-            work(odd_base(turn), (turn + 1) * n_quad, n_quad, n_quad)
-            mate_copy(turn + 1).start()
+            work(odd_of(turn), odd_base(turn), n_quad, n_quad)
+
+            @pl.when(turn < chips - 2)
+            def _():
+                mate_copy(turn + 1).start()
+
+            @pl.when(turn == chips - 2)
+            def _():
+                own_sum(chips - 2)
+                for copy in direct_copies():
+                    copy.start()
+
             for copy in fetch_odd(turn + 1):
                 copy.start()
 
         @pl.when(turn == chips - 1)
         def _():
-            work(odd_base(turn), (2 * chips - 1) * n_quad, n_quad, n_quad - 1)
+            work(odd_of(turn), odd_base(turn), n_quad, n_quad - 1)
             own_sum(chips - 1)
 
         return carry
 
     lax.fori_loop(0, chips, turns, 0)
-    for k in range(chips):
-        mate_copy(k).wait_send()
-    for k in range(chips - 1):
-        chip_copy(k).wait()
+    for k in range(chips - 2):
+        chip_copy(k).wait_recv()
 
     def add_row(to):
         total = sums[(chips - 1) * n_quad + to]
-        for k in range(chips - 1):
+        for k in range(chips - 2):
             total = total + wide_in[k, to]
         row[to] = total
 
@@ -350,9 +388,13 @@
     add_row(quad)
     for copy in copies:
         copy.wait()
+    for copy in direct_arrivals():
+        copy.wait_recv()
     total = row[quad]
     for k in range(n_quad - 1):
         total = total + quad_in[k]
+    for k in range(n_quad):
+        total = total + direct_in[k]
     end = jnp.concatenate([total[lines * cols + i : lines * cols + i + 1] for i in range(lines)], axis=1)
     total = jnp.concatenate([total[i * cols : (i + 1) * cols] for i in range(lines)], axis=1)
     sketch[:cols, :] = total
@@ -374,20 +416,28 @@
                 turned = pltpu.roll(turned, (tile - q) % n_quad * span, 1)
             packed = jnp.where(block == tile, turned, packed)
         own_gram[q] = packed
-    copies = [send(own_gram.at[peer[1]], quad_gram.at[k], peer) for k, peer in enumerate(quad_peers)]
+    swap = send(own_gram, mate_gram, mate)
+    for k in range(chips):
+        mate_copy(k).wait_send()
+    for k in range(chips - 2):
+        chip_copy(k).wait_send()
+    for copy in direct_copies():
+        copy.wait_send()
+    swap.wait()
+    pair_gram[...] = own_gram[...] + mate_gram[...]
+    copies = [
+        send(pair_gram.at[peer[1]], gram_in.at[i], peer)
+        for i, peer in reversed(list(enumerate(peers))) if i
+    ]
+    gram_in[0] = pair_gram[quad]
     for copy in copies:
         copy.wait()
-    packed = own_gram[quad]
-    for k in range(n_quad - 1):
-        packed = packed + quad_gram[k]
-    wide_gram[0] = packed
-    copies = [send(wide_gram.at[0], wide_gram.at[k + 1], peer) for k, peer in enumerate(wide_peers)]
-    for copy in copies:
-        copy.wait()
-    packed = wide_gram[wide]
-    for w in range(1, n_wide):
-        packed = packed + wide_gram[(wide + n_wide - w) % n_wide]
-    gram[...] = packed
+    total = jnp.zeros((8, LANES), jnp.float32)
+    for i in range(chips):
+        for k in range(n_quad):
+            at = ((chip - i) & (chips - 1)) * n_quad + ((quad - k) & (n_quad - 1))
+            total = total + gram_in[at]
+    gram[...] = total
 
 
 def finish_kernel(sketch_in, gram_in, sketch, gram):
@@ -418,11 +468,11 @@
     kept = LANES // (cols + 1)
     blocks = mids + -(-mids // kept)
     spaces = [
-        (devices, *packed), (half, *packed), (half, *packed), (chips - 1, n_quad, *packed),
-        (n_quad, *packed), (n_quad - 1, *packed),
-        (n_wide, *flat), (n_quad, *flat), (n_quad - 1, *flat),
+        (devices, *packed), (half, *packed), (half, *packed), (chips - 2, n_quad, *packed),
+        (n_quad, *packed), (n_quad, *packed), (n_quad - 1, *packed),
+        (n_quad, *flat), (n_quad, *flat), (n_quad, *flat), (half, *flat),
     ]
-    copies = [chips, chips - 1, 2 * (n_quad - 1) + n_wide - 1]
+    copies = [chips, chips - 2, n_quad, n_quad + half - 1]
     sketch, gram = pl.pallas_call(
         functools.partial(sketch_kernel, n_wide, n_quad, scale),
         out_shape=(
@@ -461,7 +511,7 @@
         + [pltpu.VMEM(space, f32) for space in spaces]
         + [pltpu.SemaphoreType.DMA((n,)) for n in copies for _ in range(2)],
         compiler_params=pltpu.CompilerParams(
-            vmem_limit_bytes=60 * 1024 * 1024, collective_id=0, has_side_effects=True
+            vmem_limit_bytes=56510000, collective_id=0, has_side_effects=True
         ),
     )(
         samples.reshape(-1, LANES),
@@ -478,6 +528,7 @@
         ),
         in_specs=[vmem, vmem],
         out_specs=(vmem, vmem),
+        compiler_params=pltpu.CompilerParams(vmem_limit_bytes=1024 * 1024),
     )(sketch, gram)
     return sketch.T, gram
 

time: 33.1 us -> 30.5 us (0.921)
  Pallas kernels: 32.3 us -> 29.7 us
    pallas_call x1, Pallas kernels: 30.8 us -> 28.9 us  [shards(): pl.pallas_call(functools.partial(sketch_kernel, n_wide, n_quad, scale), o...]
    pallas_call x1, Pallas kernels: 1.51 us -> 0.77 us  [shards(): pl.pallas_call(finish_kernel, out_shape=(jax.ShapeDtypeStruct((cols + 1,...]
where the time goes in v3:
time: 30.5 us; the launch traced here: 30.3 us
  Pallas kernels  29.7 us (97%)
  between operations  0.64 us (2%)
    pallas_call x1, Pallas kernels, shards(): pl.pallas_call(functools.partial(sketch_kernel, n_wide, n_quad, scale), o...  28.9 us
    pallas_call x1, Pallas kernels, shards(): pl.pallas_call(finish_kernel, out_shape=(jax.ShapeDtypeStruct((cols + 1,...  0.77 us

profile of v3, /device:TPU:0, one launch (start us, length us, event | category | flops | bytes accessed | tf_op | source)
XLA Modules:
  0.0 30.3 jit_solution(7762509692246717671)
XLA Ops:
  0.6 28.9 %shard_map.68 = (f32[17,256]{1,0:T(8,128)S(1)}, f32[8,128]{1,0:T(8,128)S(1)}) custom-call(s32[64,128]{1,0:T(8,128)} %bitcast.7, s32[64,128]{1,0:T(8,128)} %bitcast.8, s32[512,128]{1,0:T(8,128)} %bitcast.5, f32[16,65536]{1,0:T(8,128)} %x_in.1, f32[512,128]{1,0:T(8,128)} %bitcast.6), custom_call_target="tpu_custom_call" | custom-call | tf_op jit(solution)/shard_map/pallas_call | solution.py:476
  29.6 0.8 %shard_map.69 = (f32[17,256]{1,0:T(8,128)}, f32[2,16,17]{2,1,0:T(8,128)}) custom-call(f32[17,256]{1,0:T(8,128)S(1)} %get-tuple-element.6.sketch_in, f32[8,128]{1,0:T(8,128)S(1)} %get-tuple-element.7.gram_in), custom_call_target="tpu_custom_call" | custom-call | tf_op jit(solution)/shard_map/pallas_call | solution.py:523

commit v4 on v3

--- a/solution.py
+++ b/solution.py
@@ -71,10 +71,10 @@
     core, chip, chips = wide % 2, wide // 2, n_wide // 2
     mate = (wide + 1 - 2 * core, quad)
     peers = [
-        (((chip + i) & (chips - 1)) * 2 + core, (quad + k) & (n_quad - 1))
+        ((chip ^ i) * 2 + core, quad ^ k)
         for i in range(chips) for k in range(n_quad)
     ]
-    quad_peers = peers[1:n_quad]
+    quad_peers = [(wide, quad ^ k) for k in range(n_quad - 1, 0, -1)]
     barrier = pltpu.get_barrier_semaphore()
 
     def loads(h):
@@ -129,11 +129,11 @@
         return (chip_at(group) * 2 + to_core) * n_quad
 
     def even_of(turn):
-        inner = (turn > 0) & (turn < chips - 1)
-        return jnp.where(inner, turn - 1, jnp.minimum(turn, chips - 1)), jnp.where(inner, 1, 0)
+        turn = jnp.minimum(turn, chips - 1)
+        return jnp.maximum(turn - 1, 0), jnp.minimum(turn, 1)
 
     def odd_of(turn):
-        own = turn >= chips - 2
+        own = turn >= chips - 1
         return jnp.where(own, turn, turn + 1), jnp.where(own, 1, 0)
 
     def even_base(turn):
@@ -226,7 +226,7 @@
         change(blocks, pl.multiple_of(pair * 2 * LINE, 2 * LINE))
         return carry
 
-    lax.fori_loop(0, mids // 2, mix, 0, unroll=4)
+    lax.fori_loop(0, mids // 2, mix, 0, unroll=16)
     for first in range(0, spill_blocks, 2):
         blocks = []
         for i in range(first, min(first + 2, spill_blocks)):
@@ -282,10 +282,10 @@
         far = chips - 2
         return [
             remote(
-                sums.at[far * n_quad + k], direct_in.at[quad], direct_sends.at[k], direct_recvs.at[quad],
-                (chip_at(far) * 2 + core, k),
+                sums.at[far * n_quad + (quad ^ k)], direct_in.at[k], direct_sends.at[k], direct_recvs.at[k],
+                (chip_at(far) * 2 + core, quad ^ k),
             )
-            for k in range(n_quad)
+            for k in range(n_quad - 1, -1, -1)
         ]
 
     def direct_arrivals():
@@ -301,7 +301,6 @@
 
     first_fetch.wait()
     gather(2 * n_quad, 0)
-    pl.semaphore_wait(barrier, len(peers))
     owners_copy.wait()
 
     def work(step, base, buf, count):
@@ -319,6 +318,7 @@
 
         @pl.when(turn == 0)
         def _():
+            pl.semaphore_wait(barrier, len(peers))
             mate_copy(0).start()
 
         @pl.when((turn > 0) & (turn < chips - 1))
@@ -328,7 +328,9 @@
 
         @pl.when(turn == chips - 1)
         def _():
-            mate_copy(chips - 1).start()
+            own_sum(chips - 2)
+            for copy in direct_copies():
+                copy.start()
 
         @pl.when(turn < chips - 1)
         def _():
@@ -342,16 +344,7 @@
         def _():
             work(odd_of(turn), odd_base(turn), n_quad, n_quad)
 
-            @pl.when(turn < chips - 2)
-            def _():
-                mate_copy(turn + 1).start()
-
-            @pl.when(turn == chips - 2)
-            def _():
-                own_sum(chips - 2)
-                for copy in direct_copies():
-                    copy.start()
-
+            mate_copy(turn + 1).start()
             for copy in fetch_odd(turn + 1):
                 copy.start()
 
@@ -387,7 +380,8 @@
         copies.append(send(row.at[peer[1]], quad_in.at[k], peer))
     add_row(quad)
     for copy in copies:
-        copy.wait()
+        copy.wait_recv()
+    sent = copies
     for copy in direct_arrivals():
         copy.wait_recv()
     total = row[quad]
@@ -417,13 +411,8 @@
             packed = jnp.where(block == tile, turned, packed)
         own_gram[q] = packed
     swap = send(own_gram, mate_gram, mate)
-    for k in range(chips):
-        mate_copy(k).wait_send()
-    for k in range(chips - 2):
-        chip_copy(k).wait_send()
-    for copy in direct_copies():
-        copy.wait_send()
-    swap.wait()
+    swap.wait_recv()
+    sent.append(swap)
     pair_gram[...] = own_gram[...] + mate_gram[...]
     copies = [
         send(pair_gram.at[peer[1]], gram_in.at[i], peer)
@@ -431,13 +420,21 @@
     ]
     gram_in[0] = pair_gram[quad]
     for copy in copies:
-        copy.wait()
+        copy.wait_recv()
     total = jnp.zeros((8, LANES), jnp.float32)
     for i in range(chips):
         for k in range(n_quad):
-            at = ((chip - i) & (chips - 1)) * n_quad + ((quad - k) & (n_quad - 1))
+            at = (chip ^ i) * n_quad + (quad ^ k)
             total = total + gram_in[at]
     gram[...] = total
+    for k in range(chips):
+        mate_copy(k).wait_send()
+    for k in range(chips - 2):
+        chip_copy(k).wait_send()
+    for copy in direct_copies():
+        copy.wait_send()
+    for copy in sent + copies:
+        copy.wait_send()
 
 
 def finish_kernel(sketch_in, gram_in, sketch, gram):

time: 30.5 us -> 28 us (0.918)
  Pallas kernels: 29.7 us -> 27.2 us
    pallas_call x1, Pallas kernels: 28.9 us -> 26.4 us  [shards(): pl.pallas_call(functools.partial(sketch_kernel, n_wide, n_quad, scale), o...]
where the time goes in v4:
time: 28 us; the launch traced here: 27.8 us
  Pallas kernels  27.2 us (97%)
  between operations  0.64 us (2%)
    pallas_call x1, Pallas kernels, shards(): pl.pallas_call(functools.partial(sketch_kernel, n_wide, n_quad, scale), o...  26.4 us
    pallas_call x1, Pallas kernels, shards(): pl.pallas_call(finish_kernel, out_shape=(jax.ShapeDtypeStruct((cols + 1,...  0.77 us

profile of v4, /device:TPU:0, one launch (start us, length us, event | category | flops | bytes accessed | tf_op | source)
XLA Modules:
  0.0 27.8 jit_solution(11298428668192456544)
XLA Ops:
  0.6 26.4 %shard_map.68 = (f32[17,256]{1,0:T(8,128)S(1)}, f32[8,128]{1,0:T(8,128)S(1)}) custom-call(s32[64,128]{1,0:T(8,128)} %bitcast.7, s32[64,128]{1,0:T(8,128)} %bitcast.8, s32[512,128]{1,0:T(8,128)} %bitcast.5, f32[16,65536]{1,0:T(8,128)} %x_in.1, f32[512,128]{1,0:T(8,128)} %bitcast.6), custom_call_target="tpu_custom_call" | custom-call | tf_op jit(solution)/shard_map/pallas_call | solution.py:473
  27.0 0.8 %shard_map.69 = (f32[17,256]{1,0:T(8,128)}, f32[2,16,17]{2,1,0:T(8,128)}) custom-call(f32[17,256]{1,0:T(8,128)S(1)} %get-tuple-element.6.sketch_in, f32[8,128]{1,0:T(8,128)S(1)} %get-tuple-element.7.gram_in), custom_call_target="tpu_custom_call" | custom-call | tf_op jit(solution)/shard_map/pallas_call | solution.py:520

commit v5 on v4

--- a/solution.py
+++ b/solution.py
@@ -398,7 +398,12 @@
     first = lax.broadcasted_iota(jnp.int32, (8, per_dev), 0) == 0
     right = jnp.concatenate([total, jnp.where(first, end, 0.0)], axis=0)
     left = jnp.concatenate([jnp.where(group == g, total, 0.0) for g in range(GROUPS)], axis=0)
-    part = contract_last(right, left, precision=lax.Precision.HIGHEST)
+    right_top, right_low = split(right)
+    left_top, left_low = split(left)
+    part = contract_last(
+        jnp.concatenate([right_top, right_top, right_low], axis=1),
+        jnp.concatenate([left_top, left_low, left_top], axis=1),
+    )
     part = part * (GROUPS / (per_dev * devices))
     span = GROUPS * cols // n_quad
     block = lax.broadcasted_iota(jnp.int32, (8, LANES), 1) // span

time: 28 us -> 27.9 us (level)
  no operation moved by 1% of the time
where the time goes in v5:
time: 27.9 us; the launch traced here: 27.8 us
  Pallas kernels  27.1 us (97%)
  between operations  0.64 us (2%)
    pallas_call x1, Pallas kernels, shards(): pl.pallas_call(functools.partial(sketch_kernel, n_wide, n_quad, scale), o...  26.4 us
    pallas_call x1, Pallas kernels, shards(): pl.pallas_call(finish_kernel, out_shape=(jax.ShapeDtypeStruct((cols + 1,...  0.77 us

profile of v5, /device:TPU:0, one launch (start us, length us, event | category | flops | bytes accessed | tf_op | source)
XLA Modules:
  0.0 27.8 jit_solution(8918631456804732031)
XLA Ops:
  0.6 26.4 %shard_map.68 = (f32[17,256]{1,0:T(8,128)S(1)}, f32[8,128]{1,0:T(8,128)S(1)}) custom-call(s32[64,128]{1,0:T(8,128)} %bitcast.7, s32[64,128]{1,0:T(8,128)} %bitcast.8, s32[512,128]{1,0:T(8,128)} %bitcast.5, f32[16,65536]{1,0:T(8,128)} %x_in.1, f32[512,128]{1,0:T(8,128)} %bitcast.6), custom_call_target="tpu_custom_call" | custom-call | tf_op jit(solution)/shard_map/pallas_call | solution.py:478
  27.0 0.8 %shard_map.69 = (f32[17,256]{1,0:T(8,128)}, f32[2,16,17]{2,1,0:T(8,128)}) custom-call(f32[17,256]{1,0:T(8,128)S(1)} %get-tuple-element.6.sketch_in, f32[8,128]{1,0:T(8,128)S(1)} %get-tuple-element.7.gram_in), custom_call_target="tpu_custom_call" | custom-call | tf_op jit(solution)/shard_map/pallas_call | solution.py:525

commit v6 on v5

--- a/solution.py
+++ b/solution.py
@@ -122,7 +122,7 @@
     sign_of[...] = (1 - 2 * sign).astype(jnp.float32) * scale
 
     def chip_at(k):
-        return (chip + 1 + k) & (chips - 1)
+        return chip ^ (chips - 1 - k)
 
     def base_of(group, own):
         to_core = (core + 1 + own) & 1
@@ -285,7 +285,7 @@
                 sums.at[far * n_quad + (quad ^ k)], direct_in.at[k], direct_sends.at[k], direct_recvs.at[k],
                 (chip_at(far) * 2 + core, quad ^ k),
             )
-            for k in range(n_quad - 1, -1, -1)
+            for k in range(n_quad)
         ]
 
     def direct_arrivals():

time: 27.9 us -> 27.8 us (level)
  no operation moved by 1% of the time
where the time goes in v6:
time: 27.8 us; the launch traced here: 27.6 us
  Pallas kernels  27 us (97%)
  between operations  0.64 us (2%)
    pallas_call x1, Pallas kernels, shards(): pl.pallas_call(functools.partial(sketch_kernel, n_wide, n_quad, scale), o...  26.2 us
    pallas_call x1, Pallas kernels, shards(): pl.pallas_call(finish_kernel, out_shape=(jax.ShapeDtypeStruct((cols + 1,...  0.77 us

profile of v6, /device:TPU:0, one launch (start us, length us, event | category | flops | bytes accessed | tf_op | source)
XLA Modules:
  0.0 27.6 jit_solution(5170243878311568114)
XLA Ops:
  0.6 26.2 %shard_map.68 = (f32[17,256]{1,0:T(8,128)S(1)}, f32[8,128]{1,0:T(8,128)S(1)}) custom-call(s32[64,128]{1,0:T(8,128)} %bitcast.7, s32[64,128]{1,0:T(8,128)} %bitcast.8, s32[512,128]{1,0:T(8,128)} %bitcast.5, f32[16,65536]{1,0:T(8,128)} %x_in.1, f32[512,128]{1,0:T(8,128)} %bitcast.6), custom_call_target="tpu_custom_call" | custom-call | tf_op jit(solution)/shard_map/pallas_call | solution.py:478
  26.9 0.8 %shard_map.69 = (f32[17,256]{1,0:T(8,128)}, f32[2,16,17]{2,1,0:T(8,128)}) custom-call(f32[17,256]{1,0:T(8,128)S(1)} %get-tuple-element.6.sketch_in, f32[8,128]{1,0:T(8,128)S(1)} %get-tuple-element.7.gram_in), custom_call_target="tpu_custom_call" | custom-call | tf_op jit(solution)/shard_map/pallas_call | solution.py:525
